TPU v7x, 256 devices: a whole 4x4x8 slice. The times are simulated.
256 devices in a mesh: tile: 32 (over x, z_lo, core), mode: 8 (over z_hi, y).
Axes of the slice: x: 4, y: 4, z: 8 (z_hi: 2, z_lo: 4; z = z_hi * 4 + z_lo), core: 2. Of those that a mesh axis runs over, the one named last changes fastest.
Arguments:
- object_field: float32 [2, 8192, 1024], P(None, 'tile'), may hold values from -6 to 6
- probe_modes: float32 [2, 8, 256, 256], P(None, 'mode'), may hold values from -1.5 to 1.5
- measured: float32 [256, 256, 256], P('tile'), may hold values from 0.05 to 4
- row_starts: int32 [256], P('tile'), may hold values from -128 to 128, as said below
- col_starts: int32 [256], P('tile'), may hold values from 0 to 768
- live_counts: int32 [32], P('tile'), may hold values from 1 to 8, 192 in all
Outputs:
- object_grad: float32 [2, 8192, 1024], P(None, 'tile', 'mode')
- probe_grad: float32 [2, 8, 256, 256], P(None, 'mode')
Inputs may be any that keep to these rules, and one draw needn't show every extreme that they name: A window lies inside the object: on tile 0 row_starts is at least 0, on the last tile at most 0; elsewhere a window reaches at most 128 rows into the tile above or below. `live_counts`: slots of a tile from its count on are unused.
All inputs are finite; a program needn't handle non-finite values. No bound on the sum of `live_counts` on one device may be relied on, other than what follows from the above.
Results may differ from a plain program's by a relative error of at most 0.0056.
Values sent between devices are 32-bit elements; how exact they have to be, the bound alone decides.
No kernel may reach another device: no remote copies, remote signals or barrier semaphores. Data moves between devices by JAX's collectives and lax.ppermute only.
A program may use at most 64 MiB of HBM per device.

v0:
```python
import math

import jax
import jax.numpy as jnp
from jax import lax
from jax.sharding import PartitionSpec as P


def padded_2(value, sides, width):
    for axis, dim in sides:
        peers, length = (lax.axis_size(axis), value.shape[dim])
        up = [(i, (i + 1) % peers) for i in range(peers - 1)]
        down = [(j, i) for i, j in up]
        last = lax.slice_in_dim(value, length - width, length, axis=dim)
        leading = lax.slice_in_dim(value, 0, width, axis=dim)
        before = lax.ppermute(last, axis, up)
        after = lax.ppermute(leading, axis, down)
        value = jnp.concatenate([before, value, after], axis=dim)
    return value


def passed_along(value, axis, steps):
    count = lax.axis_size(axis)
    leading, last = (max(0, -steps), min(count, count - steps))
    return lax.ppermute(value, axis, [(source, source + steps) for source in range(leading, last)])


def dft_blocks(window, conj_sign):
    index_range = jnp.arange(window, dtype=jnp.int32)
    phases = index_range[:, None] * index_range[None, :] % window
    angles = phases.astype(jnp.float32) * (-2.0 * math.pi / window)
    norm_scale = 1.0 / math.sqrt(window)
    cosine_table = (jnp.cos(angles) * norm_scale).astype(jnp.bfloat16)
    sine_table = (jnp.sin(angles) * (norm_scale * conj_sign)).astype(jnp.bfloat16)
    return jnp.stack(
        [jnp.stack([cosine_table, -sine_table]), jnp.stack([sine_table, cosine_table])]
    )


def transform(wave_field, blocks_table):
    half_pass = jnp.einsum(
        "abkr,bpmrc->apmkc", blocks_table, wave_field, preferred_element_type=jnp.float32
    ).astype(jnp.bfloat16)
    return jnp.einsum(
        "bpmrc,abck->apmrk", half_pass, blocks_table, preferred_element_type=jnp.float32
    )


def complex_times(left_factor, right_factor):
    return jnp.stack(
        [
            left_factor[0] * right_factor[0] - left_factor[1] * right_factor[1],
            left_factor[0] * right_factor[1] + left_factor[1] * right_factor[0],
        ]
    )


def conj_times(left_factor, right_factor):
    return jnp.stack(
        [
            left_factor[0] * right_factor[0] + left_factor[1] * right_factor[1],
            left_factor[0] * right_factor[1] - left_factor[1] * right_factor[0],
        ]
    )


def amplitude_scaling(model_intensity, measured_block, live_block):
    floored = jnp.maximum(jnp.sqrt(model_intensity), 0.5)
    return live_block[:, None, None] * (1.0 - jnp.sqrt(measured_block) / floored)


def place_terms(accumulated, terms, row_tops, col_lefts):
    window = terms.shape[-1]
    zero_index = jnp.zeros((), jnp.int32)

    def place_one(position, current):
        anchor = (zero_index, row_tops[position], col_lefts[position])
        old_values = lax.dynamic_slice(current, anchor, (2, window, window))
        return lax.dynamic_update_slice(current, old_values + terms[:, position], anchor)

    return lax.fori_loop(0, terms.shape[1], place_one, accumulated)


def body(object_field, probe_modes, measured, row_starts, col_starts, live_counts):
    window = probe_modes.shape[-1]
    half_window = window // 2
    slot_count = row_starts.shape[0]
    tile_rows = object_field.shape[1]
    forward_blocks = dft_blocks(window, 1.0)
    backward_blocks = dft_blocks(window, -1.0)
    padded = padded_2(object_field, (("tile", 1),), half_window)
    row_tops = row_starts + half_window

    def take_patch(row_top, col_left):
        zero_index = jnp.zeros((), jnp.int32)
        return lax.dynamic_slice(padded, (zero_index, row_top, col_left), (2, window, window))

    patches = jax.vmap(take_patch, in_axes=(0, 0), out_axes=1)(row_tops, col_starts)
    live_mask = (jnp.arange(slot_count, dtype=jnp.int32) < live_counts[0]).astype(jnp.float32)
    exit_wave = complex_times(probe_modes[:, None], patches[:, :, None]).astype(jnp.bfloat16)
    far_field = transform(exit_wave, forward_blocks)
    partial_intensity = jnp.sum(far_field[0] * far_field[0] + far_field[1] * far_field[1], axis=1)
    model_intensity = lax.psum(partial_intensity, "mode")
    scaling = amplitude_scaling(model_intensity, measured, live_mask)
    residual_wave = (far_field * scaling[None, :, None]).astype(jnp.bfloat16)
    back_wave = transform(residual_wave, backward_blocks)
    object_terms = jnp.sum(conj_times(probe_modes[:, None], back_wave), axis=2)
    probe_terms = jnp.sum(conj_times(patches[:, :, None], back_wave), axis=1)
    probe_grad = lax.psum(probe_terms, "tile")
    buffer = place_terms(jnp.zeros(padded.shape, jnp.float32), object_terms, row_tops, col_starts)
    low_rim = buffer[:, :half_window]
    high_rim = buffer[:, tile_rows + half_window :]
    interior = buffer[:, half_window : half_window + tile_rows]
    from_next = passed_along(low_rim, "tile", -1)
    from_prev = passed_along(high_rim, "tile", 1)
    interior = interior.at[:, :half_window].add(from_prev)
    interior = interior.at[:, tile_rows - half_window :].add(from_next)
    object_grad = lax.psum_scatter(interior, "mode", scatter_dimension=2, tiled=True)
    return (object_grad, probe_grad)


def solution(mesh):
    return jax.shard_map(
        body,
        mesh=mesh,
        in_specs=(
            P(None, "tile", None),
            P(None, "mode", None, None),
            P("tile", None, None),
            P("tile"),
            P("tile"),
            P("tile"),
        ),
        out_specs=(P(None, "tile", "mode"), P(None, "mode", None, None)),
        check_vma=False,
    )
```

profile of v0, /device:TPU:2, one launch (start us, length us, event | category | flops | bytes accessed | tf_op | source)
XLA Modules:
  0.0 766.9 jit_solution(9628384487196969378)
XLA Ops:
  12.4 6.3 collective-permute-start.1
  23.1 13.6 %collective-permute-done = f32[2,128,1024]{2,1,0:T(8,128)} collective-permute-done((f32[2,128,1024]{2,1,0:T(8,128)}, f32[2,128,1024]{2,1,0:T(8,128)}, u32[]{:S(2)}, u32[]{:S(2)}) %collective-permute-start) | collective-permute-done | bytes 1048608 | tf_op jit(solution)/shard_map/ppermute | solution.py:16
  37.6 4.1 pad_maximum_fusion
  41.7 31.9 %while.17 = (s32[]{:T(128)}, f32[2,512,1024]{2,1,0:T(8,128)}, s32[8,3]{0,1:T(4,128)S(1)}, f32[8,2,256,256]{3,2,1,0:T(8,128)}, s32[]{:T(128)}) while((s32[]{:T(128)}, f32[2,512,1024]{2,1,0:T(8,128)}, s32[8,3]{0,1:T(4,128)S(1)}, f32[8,2,256,256]{3,2,1,0:T(8,128)}, s32[]{:T(128)}) %tuple.70), condition=%wide.while_cond.2, body=%wide.while_body.2.sunk | while | flops 2 | bytes 1050217 | solution.py:96
  73.6 5.4 copy.27
  88.6 5.9 convolution_bitcast_fusion.1
  94.5 3.8 fusion.2
  102.2 132.3 %all-reduce.3.cloned.1.call-done = f32[8,256,256]{1,2,0:T(8,128)} async-done(((f32[8,256,256]{1,2,0:T(8,128)}), f32[8,256,256]{1,2,0:T(8,128)}) %all-reduce.3.cloned.1.call-update) | async-done | bytes 2097168 | tf_op jit(solution)/shard_map/psum | solution.py:103
  234.5 4.9 subtract_multiply_fusion
  239.4 7.3 convolution_bitcast_fusion
  246.7 5.7 fusion.7
  257.3 110.6 %while.16 = (s32[]{:T(128)}, f32[2,512,1024]{2,1,0:T(8,128)}, s32[8]{0:T(128)S(1)}, s32[8]{0:T(128)S(1)}, f32[2,8,256,256]{2,3,1,0:T(8,128)}, /*index=5*/s32[]{:T(128)}, s32[]{:T(128)}, s32[]{:T(128)}, s32[]{:T(128)}) while((s32[]{:T(128)}, f32[2,512,1024]{2,1,0:T(8,128)}, s32[8]{0:T(128)S(1)}, s32[8]{0:T(128)S(1)}, ...), condition=%wide.region_2.3_spmd, body=%wide.region_1.2_spmd.sunk | while | flops 131080 | bytes 4718793 | solution.py:81
  265.0 5.6 dynamic_update_slice.8
  278.2 5.0 dynamic_update_slice.8
  291.0 6.5 dynamic_update_slice.8
  305.1 6.5 dynamic_update_slice.8
  319.4 5.5 dynamic_update_slice.8
  332.6 6.8 dynamic_update_slice.8
  347.1 6.5 dynamic_update_slice.8
  361.4 6.5 dynamic_update_slice.8
  373.2 6.6 collective-permute-start.3
  381.2 20.7 %collective-permute-done.2 = f32[2,128,1024]{2,1,0:T(8,128)} collective-permute-done((f32[2,128,1024]{2,1,0:T(8,128)}, f32[2,128,1024]{2,1,0:T(8,128)}, u32[]{:S(2)}, u32[]{:S(2)}) %collective-permute-start.2) | collective-permute-done | bytes 1048608 | tf_op jit(solution)/shard_map/ppermute | solution.py:25
  405.3 242.9 %all-reduce.5.cloned.1.call-done = f32[2,1,256,256]{2,3,0,1:T(8,128)} async-done(((f32[2,1,256,256]{2,3,0,1:T(8,128)}), f32[2,1,256,256]{2,3,0,1:T(8,128)}) %all-reduce.5.cloned.1.call-update) | async-done | bytes 524304 | tf_op jit(solution)/shard_map/psum | solution.py:109
  650.2 110.2 %reduce-scatter.2.cloned.1.call-done = f32[2,256,128]{2,1,0:T(8,128)} async-done(((f32[2,256,1024]{2,1,0:T(8,128)}), f32[2,256,128]{2,1,0:T(8,128)}) %reduce-scatter.2.cloned.1.call-update) | async-done | bytes 262160 | tf_op jit(solution)/shard_map/reduce_scatter | solution.py:118
  (125 shorter events, 102.5 us)
Async XLA Ops:
  7.2 12.6 %copy-start.6 = (f32[2,1,256,256]{3,2,1,0:T(8,128)S(1)}, f32[2,1,256,256]{3,2,1,0:T(8,128)}, u32[]{:S(2)}) copy-start(f32[2,1,256,256]{3,2,1,0:T(8,128)} %param.13) | copy-start | bytes 1572868
  7.2 227.3 %all-reduce.3.cloned.1.call-start = ((), (), s32[]{:S(2)}) async-start(), calls=%async_computation.1 | async-start | bytes 4194304 | tf_op jit(solution)/shard_map/psum | solution.py:103
  10.4 26.2 %collective-permute-start = (f32[2,128,1024]{2,1,0:T(8,128)}, f32[2,128,1024]{2,1,0:T(8,128)}, u32[]{:S(2)}, u32[]{:S(2)}) collective-permute-start(f32[2,128,1024]{2,1,0:T(8,128)} %get-tuple-element.169), channel_id=1, source_target_pairs={{0,8},{8,16},{16,24},{24,32},{32,40},{40,48},{48,56},{56,64},{64,7... | collective-permute-start | bytes 3145736 | tf_op jit(solution)/shard_map/ppermute | solution.py:16
  12.4 25.2 %collective-permute-start.1 = (f32[2,128,1024]{2,1,0:T(8,128)}, f32[2,128,1024]{2,1,0:T(8,128)}, u32[]{:S(2)}, u32[]{:S(2)}) collective-permute-start(f32[2,128,1024]{2,1,0:T(8,128)} %get-tuple-element.170), channel_id=1, source_target_pairs={{8,0},{16,8},{24,16},{32,24},{40,32},{48,40},{56,48},{64,56},{72,6... | collective-permute-start | bytes 3145736 | tf_op jit(solution)/shard_map/ppermute | solution.py:17
  19.7 3.3 copy-start.10
  19.7 3.3 copy-start.11
  19.7 17.8 %copy-start.5 = (f32[2,256,1024]{2,1,0:T(8,128)S(1)}, f32[2,256,1024]{2,1,0:T(8,128)}, u32[]{:S(2)}) copy-start(f32[2,256,1024]{2,1,0:T(8,128)} %param.12) | copy-start | bytes 6291460
  84.0 3.2 copy-start.1
  87.2 1.4 copy-start.8
  87.2 1.4 copy-start.9
  98.3 549.9 %all-reduce.5.cloned.1.call-start = ((), (), s32[]{:S(2)}) async-start(), calls=%async_computation.3 | async-start | bytes 1048576 | tf_op jit(solution)/shard_map/psum | solution.py:109
  102.2 137.2 %copy-start.7 = (bf16[1,2,256,256]{3,2,1,0:T(8,128)(2,1)S(1)}, bf16[1,2,256,256]{3,2,1,0:T(8,128)(2,1)}, u32[]{:S(2)}) copy-start(bf16[1,2,256,256]{3,2,1,0:T(8,128)(2,1)} %get-tuple-element.176) | copy-start | bytes 786436
  367.9 11.9 %copy-start = (f32[2,512,1024]{2,1,0:T(8,128)S(1)}, f32[2,512,1024]{2,1,0:T(8,128)}, u32[]{:S(2)}) copy-start(f32[2,512,1024]{2,1,0:T(8,128)} %get-tuple-element.120) | copy-start | bytes 12582916
  371.2 30.7 %collective-permute-start.2 = (f32[2,128,1024]{2,1,0:T(8,128)}, f32[2,128,1024]{2,1,0:T(8,128)}, u32[]{:S(2)}, u32[]{:S(2)}) collective-permute-start(f32[2,128,1024]{2,1,0:T(8,128)} %get-tuple-element.168), channel_id=1, source_target_pairs={{0,8},{8,16},{16,24},{24,32},{32,40},{40,48},{48,56},{56,64},{64,7... | collective-permute-start | bytes 3145736 | tf_op jit(solution)/shard_map/ppermute | solution.py:25
  373.2 6.9 copy-start.3
  373.2 6.9 copy-start.4
  373.2 30.5 %collective-permute-start.3 = (f32[2,128,1024]{2,1,0:T(8,128)}, f32[2,128,1024]{2,1,0:T(8,128)S(1)}, u32[]{:S(2)}, u32[]{:S(2)}) collective-permute-start(f32[2,128,1024]{2,1,0:T(8,128)} %get-tuple-element.167), channel_id=1, source_target_pairs={{8,0},{16,8},{24,16},{32,24},{40,32},{48,40},{56,48},{64,56},{72,6... | collective-permute-start | bytes 3145736 | tf_op jit(solution)/shard_map/ppermute | solution.py:25
  381.2 379.2 %reduce-scatter.2.cloned.1.call-start = ((), (), s32[]{:S(2)}) async-start(), calls=%async_computation.2 | async-start | bytes 2359296 | tf_op jit(solution)/shard_map/reduce_scatter | solution.py:118
  403.9 1.4 copy-start.2
Sparse Core Ops, SparseCore 0:
  98.4 135.9 all-reduce.2
  381.3 266.8 all-reduce.4
  652.8 107.5 reduce-scatter.1
where the time goes:
time: 771 us; the launch traced here: 767 us
  waiting for transfers between devices  521 us (68%)
  local copies, waits for them, and re-layouts  127 us (16%)
  other arithmetic  43.3 us (6%)
  loops' own time  31.3 us (4%)
  starting transfers between devices  17.1 us (2%)
  between operations  14.6 us (2%)
  matrix products  13.2 us (2%)
    psum x1, waiting for transfers between devices, body(): probe_grad = lax.psum(probe_terms, 'tile')  243 us
    psum x1, waiting for transfers between devices, body(): model_intensity = lax.psum(partial_intensity, 'mode')  132 us
    reduce_scatter x1, waiting for transfers between devices, body(): lax.psum_scatter(interior, 'mode', scatter_dimension=2, tiled=True)  110 us
    dynamic_update_slice x8, local copies, waits for them, and re-layouts, place_one(): lax.dynamic_update_slice(current, old_values + terms[:, position], anchor)  48.9 us
    gather x24, local copies, waits for them, and re-layouts  31.9 us
    another operation x1, loops' own time, place_terms(): return lax.fori_loop(0, terms.shape[1], place_one, accumulated)  31.2 us
    ppermute x2, waiting for transfers between devices, passed_along(): lax.ppermute(value, axis, [(source, source + steps) for source in range(l...  20.7 us
  transfers between devices with their start and end apart: 7, of which 6 were waited for; matrix products, arithmetic and copies ran while one was open for 2% of the time, Pallas kernels for 0%

commit v1 on v0

v1 whole, which is shorter than its diff:
```python
import functools
import math

import jax
import jax.numpy as jnp
import numpy as np
from jax import lax
from jax.experimental import pallas as pl
from jax.experimental.pallas import tpu as pltpu
from jax.sharding import PartitionSpec as P


WIN = 256
HALF = 128
F32 = jnp.float32
BF16 = jnp.bfloat16


def tile_perm(move):
    pairs = []
    for t in range(32):
        x, z, c = move(t // 8, t % 8 // 2, t % 2)
        pairs.append((t, x * 8 + z * 2 + c))
    return pairs


def mode_perm(move):
    pairs = []
    for m in range(8):
        z, y = move(m // 4, m % 4)
        pairs.append((m, z * 4 + y))
    return pairs


Y_PLUS = [mode_perm(lambda z, y, k=k: (z, (y + k) % 4)) for k in range(4)]
Z_SWAP = mode_perm(lambda z, y: (1 - z, y))
X_XOR = [tile_perm(lambda x, z, c, k=k: (x ^ k, z, c)) for k in range(4)]
ZLO_XOR = [tile_perm(lambda x, z, c, k=k: (x, z ^ k, c)) for k in range(4)]
CORE_SWAP = tile_perm(lambda x, z, c: (x, z, 1 - c))


def tile_step(step):
    pairs = []
    for t in range(max(0, -step), min(32, 32 - step)):
        crosses = abs(t % 8 - (t + step) % 8) == 7
        for m in range(8):
            pairs.append((t * 8 + m, (t + step) * 8 + (m ^ 4 if crosses else m)))
    return pairs


BOTH = ("tile", "mode")
TILE_UP = tile_step(1)
TILE_DOWN = tile_step(-1)


def dft_tables():
    phases = np.outer(np.arange(WIN), np.arange(WIN)) % WIN
    angles = phases * (2.0 * math.pi / WIN)
    scale = 1.0 / math.sqrt(WIN)
    cos_table = jnp.asarray((np.cos(angles) * scale).astype(np.float32)).astype(BF16)
    sin_table = jnp.asarray((-np.sin(angles) * scale).astype(np.float32)).astype(BF16)
    return cos_table, sin_table


def mm(a, b):
    return jnp.dot(a, b, preferred_element_type=F32)


def load_all(pairs, sem, first=0):
    copies = [pltpu.make_async_copy(s, d, sem.at[first + n]) for n, (s, d) in enumerate(pairs)]
    for c in copies:
        c.start()
    return copies


def wait_all(copies):
    for c in copies:
        c.wait()


def start_kernel(tile, own, probe, last, lead, part, b0, b1, b2, sem):
    core = pl.multiple_of((tile[0] & 1) * HALF, HALF)
    loads = load_all(
        [(probe.at[:, 0, pl.ds(core, HALF)], b2), (own.at[:, WIN - HALF :], b0), (own.at[:, :HALF], b1)], sem
    )
    stores = []
    for n, pair in enumerate(((b2, part), (b0, last), (b1, lead))):
        loads[n].wait()
        stores += load_all([pair], sem, 3 + n)
    wait_all(stores)


def table_kernel(cr_in, ci_in, left_out, right_out, cr_ref, ci_ref, left, right, sem):
    wait_all(load_all([(cr_in, cr_ref), (ci_in, ci_ref)], sem))
    cr, ci = cr_ref[...], ci_ref[...]
    left[:WIN, :WIN] = cr
    left[:WIN, WIN:] = -ci
    left[WIN:, :WIN] = ci
    left[WIN:, WIN:] = cr
    right[:WIN, :WIN] = cr
    right[:WIN, WIN:] = ci
    right[WIN:, :WIN] = -ci
    right[WIN:, WIN:] = cr
    wait_all(load_all([(left, left_out), (right, right_out)], sem, 2))


def two_passes(re, im, rows_table, cols_table):
    stacked = jnp.concatenate([re, im], axis=0)
    half = mm(rows_table[...], stacked).astype(BF16)
    return mm(jnp.concatenate([half[:WIN], half[WIN:]], axis=1), cols_table[...])


def probe_loads(core, p0, parts, probes):
    near = pl.multiple_of(core * HALF, HALF)
    far = pl.multiple_of((1 - core) * HALF, HALF)
    pairs = [(p0.at[:, 0], probes.at[0])]
    for j in range(3):
        pairs.append((parts[j], probes.at[j + 1, :, pl.ds(near, HALF)]))
        pairs.append((parts[3 + j], probes.at[j + 1, :, pl.ds(far, HALF)]))
    return pairs


def forward_kernel(i, mode, tile, rows, cols, left_in, right_in, above, own, below, p0, *rest):
    parts, rest = rest[:6], rest[6:]
    patch, far, inten, slab, probes, far_out, acc, out, left, right, sem_in, sem_p, sem_out = rest
    slot = (mode[0] & 3) * 2 + i
    row_top, col = rows[slot] + HALF, cols[slot]
    block = jnp.minimum(col // 128, 5)
    lane_shift = col - block * 128
    lane_start = pl.multiple_of(block * 128, 128)
    windows = load_all(
        [
            (src.at[:, :, pl.ds(lane_start, 384)], slab.at[:, pl.ds(offset, size), :])
            for src, offset, size in ((above, 0, HALF), (own, HALF, WIN), (below, HALF + WIN, HALF))
        ],
        sem_in,
    )
    loads = load_all([(left_in, left), (right_in, right)] + probe_loads(tile[0] & 1, p0, parts, probes), sem_p)
    wait_all(windows)
    row_start = pl.multiple_of(row_top // 8 * 8, 8)
    row_shift = row_top - row_start
    for part in range(2):
        tall = slab[part, pl.ds(row_start, WIN + 8), :]
        tall = pltpu.roll(tall, (WIN + 8 - row_shift) % (WIN + 8), axis=0)[:WIN]
        out[part] = pltpu.roll(tall, (384 - lane_shift) % 384, axis=1)[:, :WIN]
    wait_all(loads)
    stores = load_all([(out, patch)], sem_out)
    for j in range(4):
        pr, pi, qr, qi = probes[j, 0], probes[j, 1], out[0], out[1]
        er = (pr * qr - pi * qi).astype(BF16)
        ei = (pr * qi + pi * qr).astype(BF16)
        both = two_passes(er, ei, left, right)
        far_out[j] = both
        power = both[:, :WIN] * both[:, :WIN] + both[:, WIN:] * both[:, WIN:]
        acc[...] = power if j == 0 else acc[...] + power
        if j % 2:
            stores += load_all([(far_out.at[pl.ds(j - 1, 2)], far.at[pl.ds(j - 1, 2)])], sem_out, 1 + j // 2)
    stores += load_all([(acc, inten)], sem_out, 3)
    wait_all(stores)


def backward_kernel(i, mode, tile, rows, cols, live, left_in, right_in, mine, other, meas, patch_in, far, p0, *rest):
    parts, rest = rest[:6], rest[6:]
    if i:
        prior, rest = rest[0], rest[1:]
        rest = rest[4:]
    outs, rest = rest[:4], rest[4:]
    grads, rest = rest[: 1 + i], rest[1 + i :]
    obj, place, patch, probes, far_in, grad_out, inten, left, right, sem_i, sem_f, sem_out = rest
    core = tile[0] & 1
    y = mode[0] & 3
    slot = y * 2 + i
    row_top, col = rows[slot] + HALF, cols[slot]
    early = load_all([(mine, inten.at[0]), (other, inten.at[1]), (meas.at[slot], inten.at[2])], sem_i)
    pairs = [(left_in, left), (right_in, right), (patch_in, patch), (far, far_in)]
    pairs += probe_loads(core, p0, parts, probes)
    if i:
        pairs.append((prior, grad_out))
    loads = load_all(pairs, sem_f)
    wait_all(early)
    alive = (slot < live[0]).astype(F32)
    floored = jnp.maximum(jnp.sqrt(inten[0] + inten[1]), 0.5)
    inten[2] = alive * (1.0 - jnp.sqrt(inten[2]) / floored)
    wait_all(loads)
    stores = []
    near = pl.multiple_of(core * HALF, HALF)
    away = pl.multiple_of((1 - core) * HALF, HALF)
    for j in range(4):
        scaling = inten[2]
        xr = (far_in[j, :, :WIN] * scaling).astype(BF16)
        xi = (far_in[j, :, WIN:] * scaling).astype(BF16)
        both = two_passes(xr, xi, right, left)
        br, bi = both[:, :WIN], both[:, WIN:]
        pr, pi, qr, qi = probes[j, 0], probes[j, 1], patch[0], patch[1]
        o_r = pr * br + pi * bi
        o_i = pr * bi - pi * br
        g_r = qr * br + qi * bi
        g_i = qr * bi - qi * br
        if j == 0:
            obj[0], obj[1] = o_r, o_i
        else:
            obj[0] += o_r
            obj[1] += o_i
        if i == 0:
            grad_out[j, 0], grad_out[j, 1] = g_r, g_i
        else:
            grad_out[j, 0] += g_r
            grad_out[j, 1] += g_i
    if i == 0:
        stores += load_all([(grad_out, grads[0])], sem_out)
    else:
        stores += load_all(
            [(grad_out.at[:, :, pl.ds(near, HALF)], grads[0]), (grad_out.at[:, :, pl.ds(away, HALF)], grads[1])],
            sem_out,
        )
    block = col // 128
    lane_shift = col - block * 128
    row_shift = row_top & 7
    for part in range(2):
        wide = jnp.concatenate([obj[part], jnp.zeros((WIN, 128), F32)], axis=1)
        place[part, :WIN, :384] = pltpu.roll(wide, lane_shift, axis=1)
        place[part, WIN:, :] = jnp.zeros((8, 512), F32)
        place[part, :WIN, 384:] = jnp.zeros((WIN, 128), F32)
        for n in range(3):
            at = slice(128 * n, 128 * n + 128)
            place[part, :, at] = pltpu.roll(place[part, :, at], row_shift, axis=0)
    pairs = []
    for d, out in enumerate(outs):
        at = pl.multiple_of(((y + d - block + 8) & 3) * 128, 128)
        pairs.append((place.at[:, :, pl.ds(at, 128)], out.at[i]))
    stores += load_all(pairs, sem_out, 2)
    wait_all(stores)


def gather_kernel(mode, rows, cols, *rest):
    pieces, (mine, other, up, down, acc, buf, sem_in, sem_out) = rest[:4], rest[4:]
    loads = load_all([(p, buf.at[n]) for n, p in enumerate(pieces)], sem_in)
    acc[...] = jnp.zeros(acc.shape, F32)
    y, z_hi = mode[0] & 3, mode[0] >> 2
    wait_all(loads)
    for n in range(8):
        i, d = n % 2, n // 2
        slot = ((y + 4 - d) & 3) * 2 + i
        block = cols[slot] // 128
        low = jnp.logical_and(y >= block, y <= block + 2)
        which = jnp.where(low, 0, 1)
        start = pl.multiple_of((rows[slot] + HALF) // 8 * 8, 8)
        acc[which, :, pl.ds(start, WIN + 8), :] += buf[d, i]
    wait_all(
        load_all(
            [
                (acc.at[:, :, pl.ds(0, HALF)], up),
                (acc.at[:, :, pl.ds(HALF + WIN, HALF)], down),
                (acc.at[z_hi, :, pl.ds(HALF, WIN)], mine),
                (acc.at[1 - z_hi, :, pl.ds(HALF, WIN)], other),
            ],
            sem_out,
        )
    )


def split_kernel(tile, keep, arrived, *rest):
    outs, (total, addend, sem_in, sem_out) = rest[:4], rest[4:]
    x = tile[0] >> 3
    loads = []
    for k in range(4):
        at = pl.multiple_of((x ^ k) * 32, 32)
        pairs = [(keep.at[:, :, pl.ds(at, 32)], total.at[k]), (arrived.at[:, :, pl.ds(at, 32)], addend.at[k])]
        loads.append(load_all(pairs, sem_in, 2 * k))
    stores = []
    for k in (1, 2, 3, 0):
        wait_all(loads[k])
        total[k] += addend[k]
        stores += load_all([(total.at[k], outs[k])], sem_out, k)
    wait_all(stores)


SMEM = pl.BlockSpec(memory_space=pltpu.SMEM)
HBM = pl.BlockSpec(memory_space=pltpu.HBM)
DMA = pltpu.SemaphoreType.DMA
TABLE = (2 * WIN, 2 * WIN)


def kernel_call(kernel, scalars, arrays, outs, scratch, vmem_mib, aliases=()):
    return pl.pallas_call(
        kernel,
        out_shape=[pltpu.HBM(s, t) for s, t in outs],
        in_specs=[SMEM] * len(scalars) + [HBM] * len(arrays),
        out_specs=[HBM] * len(outs),
        scratch_shapes=scratch,
        compiler_params=pltpu.CompilerParams(vmem_limit_bytes=vmem_mib << 20),
        input_output_aliases=dict(aliases),
    )(*scalars, *arrays)


def start_call(tile, own, probe):
    shapes = [(2, HALF, 1024), (2, HALF, 1024), (2, HALF, WIN)]
    return kernel_call(start_kernel, (tile,), (own, probe), [(s, F32) for s in shapes],
        [pltpu.VMEM(s, F32) for s in shapes] + [DMA((6,))], 8)


def table_call():
    quarter = pltpu.VMEM((WIN, WIN), BF16)
    whole = pltpu.VMEM(TABLE, BF16)
    tables = [stay(t) for t in dft_tables()]
    return kernel_call(table_kernel, (), tables, [(TABLE, BF16)] * 2, [quarter, quarter, whole, whole, DMA((4,))], 6)


def forward_call(i, scalars, tables, fields, probes):
    return kernel_call(
        functools.partial(forward_kernel, i),
        scalars,
        (*tables, *fields, *probes),
        [((2, WIN, WIN), F32), ((4, WIN, 2 * WIN), F32), ((WIN, WIN), F32)],
        [
            pltpu.VMEM((2, 2 * WIN + 8, 384), F32),
            pltpu.VMEM((4, 2, WIN, WIN), F32),
            pltpu.VMEM((4, WIN, 2 * WIN), F32),
            pltpu.VMEM((WIN, WIN), F32),
            pltpu.VMEM((2, WIN, WIN), F32),
            pltpu.VMEM(TABLE, BF16),
            pltpu.VMEM(TABLE, BF16),
            DMA((3,)),
            DMA((9,)),
            DMA((4,)),
        ],
        28,
    )


def backward_call(i, scalars, tables, mine, other, measured, patch, far, probes, prior):
    window = (2, 2, WIN + 8, 128)
    grads = [((4, 2, WIN, WIN), F32)] if i == 0 else [((4, 2, HALF, WIN), F32)] * 2
    return kernel_call(
        functools.partial(backward_kernel, i),
        scalars,
        (*tables, mine, other, measured, patch, far, *probes, *prior),
        [(window, F32)] * 4 + grads,
        [
            pltpu.VMEM((2, WIN, WIN), F32),
            pltpu.VMEM((2, WIN + 8, 512), F32),
            pltpu.VMEM((2, WIN, WIN), F32),
            pltpu.VMEM((4, 2, WIN, WIN), F32),
            pltpu.VMEM((4, WIN, 2 * WIN), F32),
            pltpu.VMEM((4, 2, WIN, WIN), F32),
            pltpu.VMEM((3, WIN, WIN), F32),
            pltpu.VMEM(TABLE, BF16),
            pltpu.VMEM(TABLE, BF16),
            DMA((3,)),
            DMA((12,)),
            DMA((6,)),
        ],
        32,
        () if i == 0 else [(len(scalars) + 15 + n, n) for n in range(4)],
    )


def gather_call(scalars, pieces):
    shapes = [(2, WIN, 128), (2, WIN, 128), (2, 2, HALF, 128), (2, 2, HALF, 128)]
    return kernel_call(
        gather_kernel,
        scalars,
        pieces,
        [(s, F32) for s in shapes],
        [pltpu.VMEM((2, 2, 2 * WIN + 8, 128), F32), pltpu.VMEM((4, 2, 2, WIN + 8, 128), F32), DMA((4,)), DMA((4,))],
        16,
    )


def split_call(tile, keep, arrived):
    chunk = (4, 2, 32, WIN)
    return kernel_call(
        split_kernel,
        (tile,),
        (keep, arrived),
        [(chunk, F32)] * 4,
        [pltpu.VMEM((4, *chunk), F32), pltpu.VMEM((4, *chunk), F32), DMA((8,)), DMA((4,))],
        12,
    )


def stay(value):
    return pltpu.with_memory_space_constraint(value, pltpu.HBM)


def gradients(object_field, probe_modes, measured, row_starts, col_starts, live_counts):
    mode_index = lax.axis_index("mode").astype(jnp.int32)
    tile_index = lax.axis_index("tile").astype(jnp.int32)
    x, core = tile_index // 8, tile_index % 2
    mode, tile = mode_index.reshape(1), tile_index.reshape(1)
    scalars = (mode, tile, row_starts, col_starts)

    last, lead, part = start_call(tile, stay(object_field), stay(probe_modes))
    above = lax.ppermute(last, BOTH, TILE_UP)
    below = lax.ppermute(lead, BOTH, TILE_DOWN)
    near = [lax.ppermute(part, "mode", Y_PLUS[k]) for k in (1, 2, 3)]
    away = [lax.ppermute(near[k - 1], "tile", CORE_SWAP) for k in (1, 2, 3)]
    probes = [stay(probe_modes), *near, *away]
    tables = [stay(t) for t in table_call()]

    fields = (above, stay(object_field), below)
    fwd = [forward_call(i, scalars, tables, fields, probes) for i in range(2)]
    others = [lax.ppermute(fwd[i][2], "mode", Z_SWAP) for i in range(2)]

    prior = []
    for i in range(2):
        patch, far, mine = [stay(a) for a in fwd[i]]
        outs = backward_call(
            i, (*scalars, live_counts), tables, mine, others[i], stay(measured), patch, far, probes, prior
        )
        parts, grads = list(outs[:4]), [stay(g) for g in outs[4:]]
        prior = [*grads, *map(stay, parts)]
    pieces = [stay(parts[0])] + [lax.ppermute(parts[d], "mode", Y_PLUS[d]) for d in (1, 2, 3)]

    keep, give = grads[0], outs[5]
    arrived = lax.ppermute(give, "tile", CORE_SWAP)
    chunks = split_call(tile, keep, arrived)
    back = [lax.ppermute(chunks[k], "tile", X_XOR[k]) for k in (1, 2, 3)]
    total = (chunks[0] + back[0]) + (back[1] + back[2])
    back = [lax.ppermute(total[k], "mode", Y_PLUS[4 - k]) for k in (1, 2, 3)]
    total = (total[0] + back[0]) + (back[1] + back[2])
    back = [lax.ppermute(total, "tile", ZLO_XOR[k]) for k in (1, 2, 3)]
    total = (total + back[0]) + (back[1] + back[2])
    rows = [total] + [lax.ppermute(total, "tile", X_XOR[k]) for k in (1, 2, 3)]
    half = jnp.take(jnp.stack(rows, axis=1), jnp.arange(4) ^ x, axis=1).reshape(2, HALF, WIN)
    partner = lax.ppermute(half, "tile", CORE_SWAP)
    first = jnp.where(core == 0, half, partner)
    second = jnp.where(core == 0, partner, half)
    probe_grad = jnp.concatenate([first, second], axis=1)[:, None]

    mine, other, up, down = gather_call((mode, row_starts, col_starts), pieces)
    from_next = lax.ppermute(up, BOTH, TILE_DOWN)
    from_prev = lax.ppermute(down, BOTH, TILE_UP)
    z_hi = mode_index // 4

    def rims(which):
        above = lax.dynamic_index_in_dim(from_prev, which, 0, keepdims=False)
        below = lax.dynamic_index_in_dim(from_next, which, 0, keepdims=False)
        return jnp.concatenate([above, below], axis=1)

    crossed = lax.ppermute(other + rims(1 - z_hi), "mode", Z_SWAP)
    object_grad = (mine + rims(z_hi)) + crossed
    return (object_grad, probe_grad)


def solution(mesh):
    return jax.shard_map(
        gradients,
        mesh=mesh,
        in_specs=(
            P(None, "tile", None),
            P(None, "mode", None, None),
            P("tile", None, None),
            P("tile"),
            P("tile"),
            P("tile"),
        ),
        out_specs=(P(None, "tile", "mode"), P(None, "mode", None, None)),
        check_vma=False,
    )
```

time: 771 us -> 151 us (0.20)
  waiting for transfers between devices: 521 us -> 56.6 us
  local copies, waits for them, and re-layouts: 127 us -> 0.82 us
  other arithmetic: 43.3 us -> 1.94 us
  starting transfers between devices: 17.1 us -> 54.8 us
  Pallas kernels: 0 us -> 33.9 us
  loops' own time: 31.3 us -> 0 us
  matrix products: 13.2 us -> 0 us
  between operations: 14.6 us -> 1.65 us
    psum x2 -> x0, waiting for transfers between devices: 375 us -> none  [the longest x1 243 us: body(): probe_grad = lax.psum(probe_terms, 'tile')]
    reduce_scatter x1 -> x0, waiting for transfers between devices: 110 us -> none  [body(): lax.psum_scatter(interior, 'mode', scatter_dimension=2, tiled=True)]
    dynamic_update_slice x8 -> x0, local copies, waits for them, and re-layouts: 48.9 us -> none  [place_one(): lax.dynamic_update_slice(current, old_values + terms[:, position], anchor)]
    ppermute x4 -> x30, starting transfers between devices: 16.8 us -> 54.8 us  [the longest x1 7.18 us: gradients(): below = lax.ppermute(lead, BOTH, TILE_DOWN)]
    gather x25 -> x2, local copies, waits for them, and re-layouts: 37.3 us -> 0.58 us  [gradients(): jnp.take(jnp.stack(rows, axis=1), jnp.arange(4) ^ x, axis=1)]
    pallas_call x0 -> x8, Pallas kernels: none -> 33.9 us  [kernel_call(): pl.pallas_call(kernel, out_shape=[pltpu.HBM(s, t) for s, t in outs], in_s...]
    another operation x2 -> x0, loops' own time: 31.3 us -> none  [the longest x1 31.2 us: place_terms(): return lax.fori_loop(0, terms.shape[1], place_one, accumulated)]
    ppermute x4 -> x30, waiting for transfers between devices: 35.2 us -> 56.6 us  [the longest x3 16.2 us: gradients(): lax.ppermute(parts[d], 'mode', Y_PLUS[d])]
  transfers between devices with their start and end apart: 7 -> 30, of which waited for: 6 -> 14; matrix products, arithmetic and copies ran while one was open for 2% -> 1% of each run, Pallas kernels for 0% -> 12%
where the time goes in v1:
time: 151 us; the launch traced here: 150 us
  waiting for transfers between devices  56.6 us (37%)
  starting transfers between devices  54.8 us (36%)
  Pallas kernels  33.9 us (22%)
  other arithmetic  1.94 us (1%)
  between operations  1.65 us (1%)
    pallas_call x8, Pallas kernels, kernel_call(): pl.pallas_call(kernel, out_shape=[pltpu.HBM(s, t) for s, t in outs], in_s...  33.9 us
    ppermute x3, waiting for transfers between devices, gradients(): lax.ppermute(parts[d], 'mode', Y_PLUS[d])  16.2 us
    ppermute x2, waiting for transfers between devices, gradients(): others = [lax.ppermute(fwd[i][2], 'mode', Z_SWAP) for i in range(2)]  14 us
    ppermute x1, waiting for transfers between devices, gradients(): crossed = lax.ppermute(other + rims(1 - z_hi), 'mode', Z_SWAP)  9.85 us
    ppermute x3, waiting for transfers between devices, gradients(): near = [lax.ppermute(part, 'mode', Y_PLUS[k]) for k in (1, 2, 3)]  7.43 us
    ppermute x1, starting transfers between devices, gradients(): below = lax.ppermute(lead, BOTH, TILE_DOWN)  7.18 us
    ppermute x2, starting transfers between devices, gradients(): others = [lax.ppermute(fwd[i][2], 'mode', Z_SWAP) for i in range(2)]  6.67 us
    ppermute x3, starting transfers between devices, gradients(): near = [lax.ppermute(part, 'mode', Y_PLUS[k]) for k in (1, 2, 3)]  5.9 us
  transfers between devices with their start and end apart: 30, of which 14 were waited for; matrix products, arithmetic and copies ran while one was open for 1% of the time, Pallas kernels for 12%

profile of v1, /device:TPU:2, one launch (start us, length us, event | category | flops | bytes accessed | tf_op | source)
XLA Modules:
  0.0 149.8 jit_solution(76093176850597996)
XLA Ops:
  0.7 2.7 %shard_map.96 = (f32[2,128,1024]{2,1,0:T(8,128)}, f32[2,128,1024]{2,1,0:T(8,128)}, f32[2,128,256]{2,1,0:T(8,128)}) custom-call(s32[1]{0:T(128)} %bitcast.1.tile, f32[2,256,1024]{2,1,0:T(8,128)} %own.5, f32[2,1,256,256]{3,2,1,0:T(8,128)} %p0.7), custom_call_target="tpu_custom_call" | custom-call | tf_op jit(solution)/shard_map/pallas_call | solution.py:285
  5.3 7.2 %collective-permute-start.1 = (f32[2,128,1024]{2,1,0:T(8,128)}, f32[2,128,1024]{2,1,0:T(8,128)}, u32[]{:S(2)}, u32[]{:S(2)}) collective-permute-start(f32[2,128,1024]{2,1,0:T(8,128)} %get-tuple-element.35), channel_id=1, source_target_pairs={{8,0},{9,1},{10,2},{11,3},{12,4},{13,5},{14,6},{15,7},{16,8},{17,9... | collective-permute-start | bytes 3145736 | tf_op jit(solution)/shard_map/ppermute | solution.py:395
  14.1 2.9 %collective-permute-start.3 = (f32[2,128,256]{2,1,0:T(8,128)}, f32[2,128,256]{2,1,0:T(8,128)S(1)}, u32[]{:S(2)}, u32[]{:S(2)}) collective-permute-start(f32[2,128,256]{2,1,0:T(8,128)} %get-tuple-element.36), channel_id=1, source_target_pairs={{0,2},{1,3},{2,0},{3,1},{4,6},{5,7},{6,4},{7,5},{8,10},{9,11},{10,... | collective-permute-start | bytes 786440 | tf_op jit(solution)/shard_map/ppermute | solution.py:396
  18.4 4.6 %collective-permute-done.2.rest_0_ = f32[2,128,256]{2,1,0:T(8,128)S(1)} collective-permute-done((f32[2,128,256]{2,1,0:T(8,128)}, f32[2,128,256]{2,1,0:T(8,128)S(1)}, u32[]{:S(2)}, u32[]{:S(2)}) %collective-permute-start.2) | collective-permute-done | bytes 262176 | tf_op jit(solution)/shard_map/ppermute | solution.py:396
  23.0 2.8 %collective-permute-done.3.rest_1_ = f32[2,128,256]{2,1,0:T(8,128)S(1)} collective-permute-done((f32[2,128,256]{2,1,0:T(8,128)}, f32[2,128,256]{2,1,0:T(8,128)S(1)}, u32[]{:S(2)}, u32[]{:S(2)}) %collective-permute-start.3) | collective-permute-done | bytes 262176 | tf_op jit(solution)/shard_map/ppermute | solution.py:396
  28.4 5.1 %shard_map.98 = (f32[2,256,256]{2,1,0:T(8,128)}, f32[4,256,512]{2,1,0:T(8,128)}, f32[256,256]{1,0:T(8,128)}) custom-call(s32[1]{0:T(128)} %bitcast.mode, s32[1]{0:T(128)} %bitcast.1.tile, s32[8]{0:T(128)S(1)} %copy-done, s32[8]{0:T(128)S(1)} %copy-done.1, bf16[512,512]{1,0:T(8,128)(2,1)} %get-tuple-element.32.left_in, ...), custom_call_target="tpu_custom_call" | custom-call | tf_op jit(solution)/shard_map/pallas_call | solution.py:285
  33.6 6.4 %collective-permute-start.9 = (f32[256,256]{1,0:T(8,128)}, f32[256,256]{1,0:T(8,128)S(1)}, u32[]{:S(2)}, u32[]{:S(2)}) collective-permute-start(f32[256,256]{1,0:T(8,128)} %get-tuple-element.40.mine), channel_id=1, source_target_pairs={{0,4},{1,5},{2,6},{3,7},{4,0},{5,1},{6,2},{7,3},{8,12},{9,13},{10,... | collective-permute-start | bytes 786440 | tf_op jit(solution)/shard_map/ppermute | solution.py:403
  40.0 5.0 %shard_map.97 = (f32[2,256,256]{2,1,0:T(8,128)}, f32[4,256,512]{2,1,0:T(8,128)}, f32[256,256]{1,0:T(8,128)}) custom-call(s32[1]{0:T(128)} %bitcast.mode, s32[1]{0:T(128)} %bitcast.1.tile, s32[8]{0:T(128)S(1)} %copy-done, s32[8]{0:T(128)S(1)} %copy-done.1, bf16[512,512]{1,0:T(8,128)(2,1)} %get-tuple-element.32.left_in, ...), custom_call_target="tpu_custom_call" | custom-call | tf_op jit(solution)/shard_map/pallas_call | solution.py:285
  45.9 6.1 %collective-permute-done.9.other = f32[256,256]{1,0:T(8,128)S(1)} collective-permute-done((f32[256,256]{1,0:T(8,128)}, f32[256,256]{1,0:T(8,128)S(1)}, u32[]{:S(2)}, u32[]{:S(2)}) %collective-permute-start.9) | collective-permute-done | bytes 262176 | tf_op jit(solution)/shard_map/ppermute | solution.py:403
  52.0 6.6 %shard_map.99 = (f32[2,2,264,128]{3,2,1,0:T(8,128)}, f32[2,2,264,128]{3,2,1,0:T(8,128)}, f32[2,2,264,128]{3,2,1,0:T(8,128)}, f32[2,2,264,128]{3,2,1,0:T(8,128)}, f32[4,2,256,256]{3,2,1,0:T(8,128)}) custom-call(s32[1]{0:T(128)} %bitcast.mode, s32[1]{0:T(128)} %bitcast.1.tile, s32[8]{0:T(128)S(1)} %copy-done, s32[8]{0:T(128)S(1)} %copy-done.1, ...), custom_call_target="tpu_custom_call" | custom-call | tf_op jit(solution)/shard_map/pallas_call | solution.py:285
  58.6 7.9 %collective-permute-done.8.other = f32[256,256]{1,0:T(8,128)S(1)} collective-permute-done((f32[256,256]{1,0:T(8,128)}, f32[256,256]{1,0:T(8,128)S(1)}, u32[]{:S(2)}, u32[]{:S(2)}) %collective-permute-start.8) | collective-permute-done | bytes 262176 | tf_op jit(solution)/shard_map/ppermute | solution.py:403
  66.5 7.4 %shard_map.100 = (f32[2,2,264,128]{3,2,1,0:T(8,128)}, f32[2,2,264,128]{3,2,1,0:T(8,128)}, f32[2,2,264,128]{3,2,1,0:T(8,128)}, f32[2,2,264,128]{3,2,1,0:T(8,128)}...) custom-call(s32[1]{0:T(128)} %bitcast.mode, ...), custom_call_target="tpu_custom_call", output_to_operand_aliasing={{0}: (20, {}), {1}: (21, {}), {2}: (22, {}), {3}: (23, {})} | custom-call | tf_op jit(solution)/shard_map/pallas_call | solution.py:285
  75.3 2.4 %collective-permute-start.11 = (f32[2,2,264,128]{3,2,1,0:T(8,128)}, f32[2,2,264,128]{3,2,1,0:T(8,128)S(1)}, u32[]{:S(2)}, u32[]{:S(2)}) collective-permute-start(f32[2,2,264,128]{3,2,1,0:T(8,128)} %get-tuple-element.50), channel_id=1, source_target_pairs={{0,2},{1,3},{2,0},{3,1},{4,6},{5,7},{6,4},{7,5},{8,10},{9,11},{10,... | collective-permute-start | bytes 1622024 | tf_op jit(solution)/shard_map/ppermute | solution.py:413
  79.3 2.1 %shard_map.102 = (f32[4,2,32,256]{3,2,1,0:T(8,128)}, f32[4,2,32,256]{3,2,1,0:T(8,128)}, f32[4,2,32,256]{3,2,1,0:T(8,128)}, f32[4,2,32,256]{3,2,1,0:T(8,128)}) custom-call(s32[1]{0:T(128)} %bitcast.1.tile, f32[4,2,128,256]{3,2,1,0:T(8,128)} %get-tuple-element.56.keep, f32[4,2,128,256]{3,2,1,0:T(8,128)S(1)} %collective-permute-done.16.arrived), custom_call_target="tpu_custom_call" | custom-call | tf_op jit(solution)/shard_map/pallas_call | solution.py:285
  84.5 5.8 %collective-permute-done.10.rest_1_ = f32[2,2,264,128]{3,2,1,0:T(8,128)S(1)} collective-permute-done((f32[2,2,264,128]{3,2,1,0:T(8,128)}, f32[2,2,264,128]{3,2,1,0:T(8,128)S(1)}, u32[]{:S(2)}, u32[]{:S(2)}) %collective-permute-start.10) | collective-permute-done | bytes 540704 | tf_op jit(solution)/shard_map/ppermute | solution.py:413
  92.0 10.1 %collective-permute-done.11.rest_2_ = f32[2,2,264,128]{3,2,1,0:T(8,128)S(1)} collective-permute-done((f32[2,2,264,128]{3,2,1,0:T(8,128)}, f32[2,2,264,128]{3,2,1,0:T(8,128)S(1)}, u32[]{:S(2)}, u32[]{:S(2)}) %collective-permute-start.11) | collective-permute-done | bytes 540704 | tf_op jit(solution)/shard_map/ppermute | solution.py:413
  102.3 2.9 %shard_map.101 = (f32[2,256,128]{2,1,0:T(8,128)}, f32[2,256,128]{2,1,0:T(8,128)}, f32[2,2,128,128]{3,2,1,0:T(8,128)}, f32[2,2,128,128]{3,2,1,0:T(8,128)}) custom-call(s32[1]{0:T(128)} %bitcast.mode, s32[8]{0:T(128)S(1)} %copy-done, s32[8]{0:T(128)S(1)} %copy-done.1, f32[2,2,264,128]{3,2,1,0:T(8,128)} %get-tuple-element.48.rest_0_, ...), custom_call_target="tpu_custom_call" | custom-call | tf_op jit(solution)/shard_map/pallas_call | solution.py:285
  107.3 5.8 %collective-permute-start.14 = (f32[2,2,128,128]{3,2,1,0:T(8,128)}, f32[2,2,128,128]{3,2,1,0:T(8,128)S(1)}, u32[]{:S(2)}, u32[]{:S(2)}) collective-permute-start(f32[2,2,128,128]{3,2,1,0:T(8,128)} %get-tuple-element.54), channel_id=1, source_target_pairs={{8,0},{9,1},{10,2},{11,3},{12,4},{13,5},{14,6},{15,7},{16,8},{17,9... | collective-permute-start | bytes 786440 | tf_op jit(solution)/shard_map/ppermute | solution.py:432
  113.2 2.7 %collective-permute-start.20 = (f32[2,32,256]{2,1,0:T(8,128)S(1)}, f32[2,32,256]{2,1,0:T(8,128)S(1)}, u32[]{:S(2)}, u32[]{:S(2)}) collective-permute-start(f32[2,32,256]{2,1,0:T(8,128)S(1)} %get-tuple-element.68), channel_id=1, source_target_pairs={{0,3},{1,0},{2,1},{3,2},{4,7},{5,4},{6,5},{7,6},{8,11},{9,8},{10,9... | collective-permute-start | bytes 196616 | tf_op jit(solution)/shard_map/ppermute | solution.py:420
  117.8 3.9 %collective-permute-done.21 = f32[2,32,256]{2,1,0:T(8,128)S(1)} collective-permute-done((f32[2,32,256]{2,1,0:T(8,128)S(1)}, f32[2,32,256]{2,1,0:T(8,128)S(1)}, u32[]{:S(2)}, u32[]{:S(2)}) %collective-permute-start.21) | collective-permute-done | bytes 65568 | tf_op jit(solution)/shard_map/ppermute | solution.py:420
  123.0 4.1 %collective-permute-start.25 = (f32[2,32,256]{2,1,0:T(8,128)S(1)}, f32[2,32,256]{2,1,0:T(8,128)S(1)}, u32[]{:S(2)}, u32[]{:S(2)}) collective-permute-start(f32[2,32,256]{2,1,0:T(8,128)S(1)} %fusion.2), channel_id=1, source_target_pairs={{0,48},{8,56},{16,32},{24,40},{32,16},{40,24},{48,0},{56,8},{64,11... | collective-permute-start | bytes 196616 | tf_op jit(solution)/shard_map/ppermute | solution.py:422
  130.2 2.9 %collective-permute-start.27 = (f32[2,32,256]{2,1,0:T(8,128)S(1)}, f32[2,32,256]{2,1,0:T(8,128)S(1)}, u32[]{:S(2)}, u32[]{:S(2)}) collective-permute-start(f32[2,32,256]{2,1,0:T(8,128)S(1)} %add_add_fusion.1), channel_id=1, source_target_pairs={{0,128},{8,136},{16,144},{24,152},{32,160},{40,168},{48,176},{56,1... | collective-permute-start | bytes 196616 | tf_op jit(solution)/shard_map/ppermute | solution.py:424
  133.7 2.9 %collective-permute-start.15 = (f32[2,256,128]{2,1,0:T(8,128)S(1)}, f32[2,256,128]{2,1,0:T(8,128)S(1)}, u32[]{:S(2)}, u32[]{:S(2)}) collective-permute-start(f32[2,256,128]{2,1,0:T(8,128)S(1)} %maximum_add_fusion.1), channel_id=1, source_target_pairs={{0,4},{1,5},{2,6},{3,7},{4,0},{5,1},{6,2},{7,3},{8,12},{9,13},{10,... | collective-permute-start | bytes 786440 | tf_op jit(solution)/shard_map/ppermute | solution.py:441
  138.2 9.9 %collective-permute-done.15 = f32[2,256,128]{2,1,0:T(8,128)S(1)} collective-permute-done((f32[2,256,128]{2,1,0:T(8,128)S(1)}, f32[2,256,128]{2,1,0:T(8,128)S(1)}, u32[]{:S(2)}, u32[]{:S(2)}) %collective-permute-start.15) | collective-permute-done | bytes 262176 | tf_op jit(solution)/shard_map/ppermute | solution.py:441
  (73 shorter events, 28.0 us)
Async XLA Ops:
  3.4 25.0 %collective-permute-start = (f32[2,128,1024]{2,1,0:T(8,128)}, f32[2,128,1024]{2,1,0:T(8,128)S(1)}, u32[]{:S(2)}, u32[]{:S(2)}) collective-permute-start(f32[2,128,1024]{2,1,0:T(8,128)} %get-tuple-element.34), channel_id=1, source_target_pairs={{0,8},{1,9},{2,10},{3,11},{4,12},{5,13},{6,14},{7,15},{8,16},{9,17... | collective-permute-start | bytes 3145736 | tf_op jit(solution)/shard_map/ppermute | solution.py:394
  5.3 23.1 %collective-permute-start.1 = (f32[2,128,1024]{2,1,0:T(8,128)}, f32[2,128,1024]{2,1,0:T(8,128)}, u32[]{:S(2)}, u32[]{:S(2)}) collective-permute-start(f32[2,128,1024]{2,1,0:T(8,128)} %get-tuple-element.35), channel_id=1, source_target_pairs={{8,0},{9,1},{10,2},{11,3},{12,4},{13,5},{14,6},{15,7},{16,8},{17,9... | collective-permute-start | bytes 3145736 | tf_op jit(solution)/shard_map/ppermute | solution.py:395
  12.5 10.5 %collective-permute-start.2 = (f32[2,128,256]{2,1,0:T(8,128)}, f32[2,128,256]{2,1,0:T(8,128)S(1)}, u32[]{:S(2)}, u32[]{:S(2)}) collective-permute-start(f32[2,128,256]{2,1,0:T(8,128)} %get-tuple-element.36), channel_id=1, source_target_pairs={{0,1},{1,2},{2,3},{3,0},{4,5},{5,6},{6,7},{7,4},{8,9},{9,10},{10,1... | collective-permute-start | bytes 786440 | tf_op jit(solution)/shard_map/ppermute | solution.py:396
  14.1 11.7 %collective-permute-start.3 = (f32[2,128,256]{2,1,0:T(8,128)}, f32[2,128,256]{2,1,0:T(8,128)S(1)}, u32[]{:S(2)}, u32[]{:S(2)}) collective-permute-start(f32[2,128,256]{2,1,0:T(8,128)} %get-tuple-element.36), channel_id=1, source_target_pairs={{0,2},{1,3},{2,0},{3,1},{4,6},{5,7},{6,4},{7,5},{8,10},{9,11},{10,... | collective-permute-start | bytes 786440 | tf_op jit(solution)/shard_map/ppermute | solution.py:396
  17.0 8.8 %collective-permute-start.4 = (f32[2,128,256]{2,1,0:T(8,128)}, f32[2,128,256]{2,1,0:T(8,128)S(1)}, u32[]{:S(2)}, u32[]{:S(2)}) collective-permute-start(f32[2,128,256]{2,1,0:T(8,128)} %get-tuple-element.36), channel_id=1, source_target_pairs={{0,3},{1,0},{2,1},{3,2},{4,7},{5,4},{6,5},{7,6},{8,11},{9,8},{10,9... | collective-permute-start | bytes 786440 | tf_op jit(solution)/shard_map/ppermute | solution.py:396
  23.0 5.4 %collective-permute-start.5 = (f32[2,128,256]{2,1,0:T(8,128)S(1)}, f32[2,128,256]{2,1,0:T(8,128)S(1)}, u32[]{:S(2)}, u32[]{:S(2)}) collective-permute-start(f32[2,128,256]{2,1,0:T(8,128)S(1)} %collective-permute-done.2.rest_0_), channel_id=1, source_target_pairs={{0,8},{8,0},{16,24},{24,16},{32,40},{40,32},{48,56},{56,48},{64,72... | collective-permute-start | bytes 786440 | tf_op jit(solution)/shard_map/ppermute | solution.py:397
  33.6 18.5 %collective-permute-start.9 = (f32[256,256]{1,0:T(8,128)}, f32[256,256]{1,0:T(8,128)S(1)}, u32[]{:S(2)}, u32[]{:S(2)}) collective-permute-start(f32[256,256]{1,0:T(8,128)} %get-tuple-element.40.mine), channel_id=1, source_target_pairs={{0,4},{1,5},{2,6},{3,7},{4,0},{5,1},{6,2},{7,3},{8,12},{9,13},{10,... | collective-permute-start | bytes 786440 | tf_op jit(solution)/shard_map/ppermute | solution.py:403
  45.0 21.5 %collective-permute-start.8 = (f32[256,256]{1,0:T(8,128)}, f32[256,256]{1,0:T(8,128)S(1)}, u32[]{:S(2)}, u32[]{:S(2)}) collective-permute-start(f32[256,256]{1,0:T(8,128)} %get-tuple-element.37.mine), channel_id=1, source_target_pairs={{0,4},{1,5},{2,6},{3,7},{4,0},{5,1},{6,2},{7,3},{8,12},{9,13},{10,... | collective-permute-start | bytes 786440 | tf_op jit(solution)/shard_map/ppermute | solution.py:403
  74.0 16.3 %collective-permute-start.10 = (f32[2,2,264,128]{3,2,1,0:T(8,128)}, f32[2,2,264,128]{3,2,1,0:T(8,128)S(1)}, u32[]{:S(2)}, u32[]{:S(2)}) collective-permute-start(f32[2,2,264,128]{3,2,1,0:T(8,128)} %get-tuple-element.49), channel_id=1, source_target_pairs={{0,1},{1,2},{2,3},{3,0},{4,5},{5,6},{6,7},{7,4},{8,9},{9,10},{10,1... | collective-permute-start | bytes 1622024 | tf_op jit(solution)/shard_map/ppermute | solution.py:413
  75.3 26.8 %collective-permute-start.11 = (f32[2,2,264,128]{3,2,1,0:T(8,128)}, f32[2,2,264,128]{3,2,1,0:T(8,128)S(1)}, u32[]{:S(2)}, u32[]{:S(2)}) collective-permute-start(f32[2,2,264,128]{3,2,1,0:T(8,128)} %get-tuple-element.50), channel_id=1, source_target_pairs={{0,2},{1,3},{2,0},{3,1},{4,6},{5,7},{6,4},{7,5},{8,10},{9,11},{10,... | collective-permute-start | bytes 1622024 | tf_op jit(solution)/shard_map/ppermute | solution.py:413
  77.7 24.6 %collective-permute-start.12 = (f32[2,2,264,128]{3,2,1,0:T(8,128)}, f32[2,2,264,128]{3,2,1,0:T(8,128)S(1)}, u32[]{:S(2)}, u32[]{:S(2)}) collective-permute-start(f32[2,2,264,128]{3,2,1,0:T(8,128)} %get-tuple-element.51), channel_id=1, source_target_pairs={{0,3},{1,0},{2,1},{3,2},{4,7},{5,4},{6,5},{7,6},{8,11},{9,8},{10,9... | collective-permute-start | bytes 1622024 | tf_op jit(solution)/shard_map/ppermute | solution.py:413
  81.4 31.6 %collective-permute-start.17 = (f32[4,2,32,256]{3,2,1,0:T(8,128)}, f32[4,2,32,256]{3,2,1,0:T(8,128)S(1)}, u32[]{:S(2)}, u32[]{:S(2)}) collective-permute-start(f32[4,2,32,256]{3,2,1,0:T(8,128)} %get-tuple-element.59), channel_id=1, source_target_pairs={{0,64},{8,72},{16,80},{24,88},{32,96},{40,104},{48,112},{56,120},{... | collective-permute-start | bytes 786440 | tf_op jit(solution)/shard_map/ppermute | solution.py:418
  82.8 30.3 %collective-permute-start.18 = (f32[4,2,32,256]{3,2,1,0:T(8,128)}, f32[4,2,32,256]{3,2,1,0:T(8,128)S(1)}, u32[]{:S(2)}, u32[]{:S(2)}) collective-permute-start(f32[4,2,32,256]{3,2,1,0:T(8,128)} %get-tuple-element.60), channel_id=1, source_target_pairs={{0,128},{8,136},{16,144},{24,152},{32,160},{40,168},{48,176},{56,1... | collective-permute-start | bytes 786440 | tf_op jit(solution)/shard_map/ppermute | solution.py:418
  90.3 22.8 %collective-permute-start.19 = (f32[4,2,32,256]{3,2,1,0:T(8,128)}, f32[4,2,32,256]{3,2,1,0:T(8,128)S(1)}, u32[]{:S(2)}, u32[]{:S(2)}) collective-permute-start(f32[4,2,32,256]{3,2,1,0:T(8,128)} %get-tuple-element.61), channel_id=1, source_target_pairs={{0,192},{8,200},{16,208},{24,216},{32,224},{40,232},{48,240},{56,2... | collective-permute-start | bytes 786440 | tf_op jit(solution)/shard_map/ppermute | solution.py:418
  105.2 12.0 %collective-permute-start.13 = (f32[2,2,128,128]{3,2,1,0:T(8,128)}, f32[2,2,128,128]{3,2,1,0:T(8,128)S(1)}, u32[]{:S(2)}, u32[]{:S(2)}) collective-permute-start(f32[2,2,128,128]{3,2,1,0:T(8,128)} %get-tuple-element.53), channel_id=1, source_target_pairs={{0,8},{1,9},{2,10},{3,11},{4,12},{5,13},{6,14},{7,15},{8,16},{9,17... | collective-permute-start | bytes 786440 | tf_op jit(solution)/shard_map/ppermute | solution.py:433
  107.3 19.7 %collective-permute-start.14 = (f32[2,2,128,128]{3,2,1,0:T(8,128)}, f32[2,2,128,128]{3,2,1,0:T(8,128)S(1)}, u32[]{:S(2)}, u32[]{:S(2)}) collective-permute-start(f32[2,2,128,128]{3,2,1,0:T(8,128)} %get-tuple-element.54), channel_id=1, source_target_pairs={{8,0},{9,1},{10,2},{11,3},{12,4},{13,5},{14,6},{15,7},{16,8},{17,9... | collective-permute-start | bytes 786440 | tf_op jit(solution)/shard_map/ppermute | solution.py:432
  115.9 5.8 %collective-permute-start.21 = (f32[2,32,256]{2,1,0:T(8,128)S(1)}, f32[2,32,256]{2,1,0:T(8,128)S(1)}, u32[]{:S(2)}, u32[]{:S(2)}) collective-permute-start(f32[2,32,256]{2,1,0:T(8,128)S(1)} %get-tuple-element.67), channel_id=1, source_target_pairs={{0,2},{1,3},{2,0},{3,1},{4,6},{5,7},{6,4},{7,5},{8,10},{9,11},{10,... | collective-permute-start | bytes 196616 | tf_op jit(solution)/shard_map/ppermute | solution.py:420
  117.1 5.5 %collective-permute-start.22 = (f32[2,32,256]{2,1,0:T(8,128)S(1)}, f32[2,32,256]{2,1,0:T(8,128)S(1)}, u32[]{:S(2)}, u32[]{:S(2)}) collective-permute-start(f32[2,32,256]{2,1,0:T(8,128)S(1)} %get-tuple-element.66), channel_id=1, source_target_pairs={{0,1},{1,2},{2,3},{3,0},{4,5},{5,6},{6,7},{7,4},{8,9},{9,10},{10,1... | collective-permute-start | bytes 196616 | tf_op jit(solution)/shard_map/ppermute | solution.py:420
  122.7 5.7 %collective-permute-start.24 = (f32[2,32,256]{2,1,0:T(8,128)S(1)}, f32[2,32,256]{2,1,0:T(8,128)S(1)}, u32[]{:S(2)}, u32[]{:S(2)}) collective-permute-start(f32[2,32,256]{2,1,0:T(8,128)S(1)} %fusion.2), channel_id=1, source_target_pairs={{0,32},{8,40},{16,48},{24,56},{32,0},{40,8},{48,16},{56,24},{64,96... | collective-permute-start | bytes 196616 | tf_op jit(solution)/shard_map/ppermute | solution.py:422
  123.0 7.1 %collective-permute-start.25 = (f32[2,32,256]{2,1,0:T(8,128)S(1)}, f32[2,32,256]{2,1,0:T(8,128)S(1)}, u32[]{:S(2)}, u32[]{:S(2)}) collective-permute-start(f32[2,32,256]{2,1,0:T(8,128)S(1)} %fusion.2), channel_id=1, source_target_pairs={{0,48},{8,56},{16,32},{24,40},{32,16},{40,24},{48,0},{56,8},{64,11... | collective-permute-start | bytes 196616 | tf_op jit(solution)/shard_map/ppermute | solution.py:422
  130.1 6.5 %collective-permute-start.26 = (f32[2,32,256]{2,1,0:T(8,128)S(1)}, f32[2,32,256]{2,1,0:T(8,128)S(1)}, u32[]{:S(2)}, u32[]{:S(2)}) collective-permute-start(f32[2,32,256]{2,1,0:T(8,128)S(1)} %add_add_fusion.1), channel_id=1, source_target_pairs={{0,64},{8,72},{16,80},{24,88},{32,96},{40,104},{48,112},{56,120},{... | collective-permute-start | bytes 196616 | tf_op jit(solution)/shard_map/ppermute | solution.py:424
  130.2 6.4 %collective-permute-start.27 = (f32[2,32,256]{2,1,0:T(8,128)S(1)}, f32[2,32,256]{2,1,0:T(8,128)S(1)}, u32[]{:S(2)}, u32[]{:S(2)}) collective-permute-start(f32[2,32,256]{2,1,0:T(8,128)S(1)} %add_add_fusion.1), channel_id=1, source_target_pairs={{0,128},{8,136},{16,144},{24,152},{32,160},{40,168},{48,176},{56,1... | collective-permute-start | bytes 196616 | tf_op jit(solution)/shard_map/ppermute | solution.py:424
  133.7 14.4 %collective-permute-start.15 = (f32[2,256,128]{2,1,0:T(8,128)S(1)}, f32[2,256,128]{2,1,0:T(8,128)S(1)}, u32[]{:S(2)}, u32[]{:S(2)}) collective-permute-start(f32[2,256,128]{2,1,0:T(8,128)S(1)} %maximum_add_fusion.1), channel_id=1, source_target_pairs={{0,4},{1,5},{2,6},{3,7},{4,0},{5,1},{6,2},{7,3},{8,12},{9,13},{10,... | collective-permute-start | bytes 786440 | tf_op jit(solution)/shard_map/ppermute | solution.py:441
  138.1 10.7 %collective-permute-start.29 = (f32[2,128,256]{2,1,0:T(8,128)S(1)}, f32[2,128,256]{2,1,0:T(8,128)S(1)}, u32[]{:S(2)}, u32[]{:S(2)}) collective-permute-start(f32[2,128,256]{2,1,0:T(8,128)S(1)} %bitcast_select_fusion), channel_id=1, source_target_pairs={{0,8},{8,0},{16,24},{24,16},{32,40},{40,32},{48,56},{56,48},{64,72... | collective-permute-start | bytes 786440 | tf_op jit(solution)/shard_map/ppermute | solution.py:426
  (11 other events, 170.4 us)
